TPU v7x, 256 devices: a whole 4x4x8 slice. The times are simulated.
256 devices in a mesh: row: 16 (over x_lo, z), col: 4 (over x_hi, core), slab: 4 (over y).
Axes of the slice: x: 4 (x_hi: 2, x_lo: 2; x = x_hi * 2 + x_lo), y: 4, z: 8, core: 2. Of those that a mesh axis runs over, the one named last changes fastest.
Arguments:
- inputs: bfloat16 [32, 64, 6144], P('col', None, ('row', 'slab')), may hold values from -6 to 6
- first_weight: bfloat16 [3, 3, 6144, 6144], P(None, None, ('row', 'slab'), 'col'), may hold values from -0.02734375 to 0.02734375
- second_weight: bfloat16 [3, 3, 6144, 6144], P(None, None, 'col', ('row', 'slab')), may hold values from -0.02734375 to 0.02734375
Outputs:
- result: bfloat16 [32, 64, 6144], P('col', None, ('row', 'slab'))
All inputs are finite; a program needn't handle non-finite values.
Results may differ from a plain program's by a relative error of at most 0.015.
Values may be sent and summed in bfloat16 or wider, within the bound.
No kernel may reach another device: no remote copies, remote signals or barrier semaphores. Data moves between devices by JAX's collectives and lax.ppermute only.
A program may use at most 128 MiB of HBM per device.

v0:
```python
import jax
import jax.numpy as jnp
from jax import lax
from jax.sharding import PartitionSpec as P


def local(inputs, first_weight, second_weight):
    full_input = lax.all_gather(inputs, "col", axis=0, tiled=True)
    height = full_input.shape[0]
    width = full_input.shape[1]
    pixels = height * width
    row_count = lax.axis_size("row")
    slab_count = lax.axis_size("slab")
    block = pixels // (row_count * slab_count)
    out_first = first_weight.shape[3]
    channels = lax.all_gather(full_input, "slab", axis=2, tiled=True)
    kernel = lax.all_gather(first_weight, "slab", axis=2, tiled=True)
    padded = jnp.pad(channels, ((1, 1), (1, 1), (0, 0)))
    position = lax.axis_index("slab")
    partial_sum = jnp.zeros((row_count * block, out_first), jnp.float32)
    for vertical in range(3):
        for sideways in range(3):
            window = padded[vertical : vertical + height, sideways : sideways + width, :]
            window = window.reshape(row_count, slab_count, block, channels.shape[2])
            chosen = lax.dynamic_index_in_dim(window, position, 1, keepdims=False)
            chosen = chosen.reshape(row_count * block, channels.shape[2])
            partial_sum = partial_sum + jnp.dot(
                chosen, kernel[vertical, sideways], preferred_element_type=jnp.float32
            )
    first = lax.psum_scatter(
        partial_sum.astype(jnp.bfloat16), "row", scatter_dimension=0, tiled=True
    ).astype(jnp.float32)
    hidden = jax.nn.silu(first).astype(jnp.bfloat16)
    gathered = lax.all_gather(hidden, ("row", "slab"), axis=0, tiled=True)
    padded_hidden = jnp.pad(gathered.reshape(height, width, out_first), ((1, 1), (1, 1), (0, 0)))
    rows_out = pixels // lax.axis_size("col")
    out_second = second_weight.shape[3]
    lines = rows_out * lax.axis_size("col") // width
    total = jnp.zeros((rows_out * lax.axis_size("col"), out_second), jnp.float32)
    for vertical in range(3):
        for sideways in range(3):
            window = padded_hidden[
                vertical : vertical + lines, sideways : sideways + width, :
            ].reshape(rows_out * lax.axis_size("col"), out_first)
            total = total + jnp.dot(
                window, second_weight[vertical, sideways], preferred_element_type=jnp.float32
            )
    second = lax.psum_scatter(
        total.astype(jnp.bfloat16), "col", scatter_dimension=0, tiled=True
    ).astype(jnp.float32)
    combined = inputs.astype(jnp.float32) + second.reshape(inputs.shape)
    return combined.astype(jnp.bfloat16)


def solution(mesh):
    in_specs = (
        P("col", None, ("row", "slab")),
        P(None, None, ("row", "slab"), "col"),
        P(None, None, "col", ("row", "slab")),
    )
    out_specs = P("col", None, ("row", "slab"))
    return jax.shard_map(local, mesh=mesh, in_specs=in_specs, out_specs=out_specs, check_vma=False)
```

profile of v0, /device:TPU:1, one launch (start us, length us, event | category | flops | bytes accessed | tf_op | source)
XLA Modules:
  0.0 662.9 jit_solution(12027677291093433866)
XLA Ops:
  6.5 0.0 all-gather.4.cloned.1.call-start
  6.5 11.2 %all_gather.12 = bf16[32,64,96]{2,1,0:T(8,128)(2,1)S(1)} all-gather(bf16[8,64,96]{2,1,0:T(8,128)(2,1)} %param.3), channel_id=1, replica_groups=mesh['row'=16,'col'=4,'slab'=4] {'col'}, dimensions={0}, use_global_device_ids=true | all-gather | bytes 491520 | tf_op jit(solution)/shard_map/all_gather | solution.py:8
  17.8 2.1 copy.8
  19.8 0.0 all-gather.4.cloned.1.call-update
  19.9 0.0 all-gather.6.cloned.1.call-start
  19.9 0.7 all-gather.6.cloned.1.call-update
  20.6 0.0 reduce-scatter.3.cloned.1.call-start
  20.7 42.3 %all-gather.4.cloned.1.call-done = bf16[32,64,384]{1,0,2:T(8,128)(2,1)} async-done(((bf16[32,64,96]{1,0,2:T(8,128)(2,1)}), bf16[32,64,384]{1,0,2:T(8,128)(2,1)}) %all-gather.4.cloned.1.call-update) | async-done | bytes 1572880 | tf_op jit(solution)/shard_map/all_gather | solution.py:16
  62.9 4.6 copy.9
  67.5 5.1 pad_slice_fusion.8
  72.6 0.1 constant_dynamic-slice_fusion.8
  72.7 0.1 constant_dynamic-slice_fusion.4
  72.8 0.1 constant_dynamic-slice_fusion
  72.9 0.1 constant_dynamic-slice_fusion.6
  73.0 0.1 constant_dynamic-slice_fusion.2
  73.1 96.3 %all-gather.6.cloned.1.call-done = bf16[3,3,384,1536]{3,2,1,0:T(8,128)(2,1)} async-done(((bf16[3,3,96,1536]{3,2,1,0:T(8,128)(2,1)}), bf16[3,3,384,1536]{3,2,1,0:T(8,128)(2,1)}) %all-gather.6.cloned.1.call-update) | async-done | bytes 10616848 | tf_op jit(solution)/shard_map/all_gather | solution.py:17
  169.4 2.4 fusion.2
  171.8 2.9 convolution_add_fusion.7
  174.7 0.0 copy-done.1
  174.7 1.0 convolution_add_fusion.6
  175.7 1.0 convolution_add_fusion.5
  176.8 1.0 convolution_add_fusion.4
  177.8 1.0 convolution_add_fusion.3
  178.8 1.0 convolution_add_fusion.2
  179.8 1.0 convolution_add_fusion.1
  180.8 2.2 fusion
  183.0 0.0 reduce-scatter.3.cloned.1.call-update
  183.0 0.0 all-gather.8.cloned.1.call-start
  183.1 63.6 %reduce-scatter.3.cloned.1.call-done = bf16[32,1536]{1,0:T(8,128)(2,1)} async-done(((bf16[512,1536]{1,0:T(8,128)(2,1)}), bf16[32,1536]{1,0:T(8,128)(2,1)}) %reduce-scatter.3.cloned.1.call-update) | async-done | bytes 98320 | tf_op jit(solution)/shard_map/reduce_scatter | solution.py:30
  246.7 1.6 fusion.25
  248.3 0.0 all-gather.8.cloned.1.call-update
  248.3 0.2 reduce-scatter.5.cloned.1.call-start
  248.5 269.5 %all-gather.8.cloned.1.call-done = bf16[2048,1536]{1,0:T(8,128)(2,1)} async-done(((bf16[32,1536]{1,0:T(8,128)(2,1)}), bf16[2048,1536]{1,0:T(8,128)(2,1)}) %all-gather.8.cloned.1.call-update) | async-done | bytes 6291472 | tf_op jit(solution)/shard_map/all_gather | solution.py:34
  518.0 37.0 %pad_slice_fusion = (bf16[32,64,1536]{2,1,0:T(8,128)(2,1)}, bf16[32,64,1536]{2,1,0:T(8,128)(2,1)}, bf16[32,64,1536]{2,1,0:T(8,128)(2,1)}, bf16[32,64,1536]{2,1,0...) fusion(bf16[32,64,1536]{2,1,0:T(8,128)(2,1)} %bitcast.100), kind=kLoop, calls=%fused_computation | loop fusion | bytes 56623104 | tf_op jit(solution)/shard_map/slice | solution.py:42
  555.0 0.0 copy-done.2
  555.0 0.0 copy-start
  555.0 0.0 slice-start.10
  555.1 4.9 fusion.11
  560.0 0.0 slice-start.11
  560.0 5.0 convolution_add_fusion.15
  565.0 0.0 copy-done
  565.0 0.0 slice-start
  565.0 0.0 slice-start.8
  565.0 2.0 convolution_add_fusion.14
  567.0 0.0 slice-start.1
  567.0 0.0 slice-done.10
  567.0 0.0 slice-done.11
  567.1 0.0 slice-start.9
  567.1 0.0 slice-start.6
  567.1 2.0 convolution_add_fusion.13
  569.1 0.1 slice-done.1
  569.2 2.0 convolution_add_fusion.12
  571.3 0.0 slice-start.5
  571.3 2.0 convolution_add_fusion.11
  573.4 0.0 slice-start.2
  573.4 2.0 convolution_add_fusion.10
  575.4 0.0 slice-start.3
  575.4 2.0 convolution_add_fusion.9
  577.5 0.0 copy-start.3
  577.5 2.8 fusion.1
  580.3 0.0 reduce-scatter.5.cloned.1.call-update
  580.3 74.4 %reduce-scatter.5.cloned.1.call-done = bf16[512,96]{0,1:T(8,128)(2,1)} async-done(((bf16[2048,96]{0,1:T(8,128)(2,1)}), bf16[512,96]{0,1:T(8,128)(2,1)}) %reduce-scatter.5.cloned.1.call-update) | async-done | bytes 98320 | tf_op jit(solution)/shard_map/reduce_scatter | solution.py:48
  654.6 1.0 copy.11
  655.7 0.7 add_convert_fusion
  (20 shorter events, 0.0 us)
Async XLA Ops:
  6.5 56.4 %all-gather.4.cloned.1.call-start = ((), (), s32[]{:S(2)}) async-start(), calls=%async_computation.2 | async-start | bytes 3932160 | tf_op jit(solution)/shard_map/all_gather | solution.py:16
  19.9 149.6 %all-gather.6.cloned.1.call-start = ((), (), s32[]{:S(2)}) async-start(), calls=%async_computation.3 | async-start | bytes 13271040 | tf_op jit(solution)/shard_map/all_gather | solution.py:17
  20.6 226.1 %reduce-scatter.3.cloned.1.call-start = ((), (), s32[]{:S(2)}) async-start(), calls=%async_computation.4 | async-start | bytes 1671168 | tf_op jit(solution)/shard_map/reduce_scatter | solution.py:30
  169.4 5.3 copy-start.1
  183.0 335.0 %all-gather.8.cloned.1.call-start = ((), (), s32[]{:S(2)}) async-start(), calls=%async_computation.5 | async-start | bytes 6389760 | tf_op jit(solution)/shard_map/all_gather | solution.py:34
  248.3 406.3 %reduce-scatter.5.cloned.1.call-start = ((), (), s32[]{:S(2)}) async-start(), calls=%async_computation.6 | async-start | bytes 491520 | tf_op jit(solution)/shard_map/reduce_scatter | solution.py:48
  518.0 37.0 %copy-start.2 = (bf16[3,3,1536,96]{2,3,1,0:T(8,128)(2,1)S(1)}, bf16[3,3,1536,96]{2,3,1,0:T(8,128)(2,1)}, u32[]{:S(2)}) copy-start(bf16[3,3,1536,96]{2,3,1,0:T(8,128)(2,1)} %param.5) | copy-start | bytes 7962628
  555.0 9.9 %copy-start = (bf16[32,64,1536]{2,1,0:T(8,128)(2,1)S(1)}, bf16[32,64,1536]{2,1,0:T(8,128)(2,1)}, u32[]{:S(2)}) copy-start(bf16[32,64,1536]{2,1,0:T(8,128)(2,1)} %get-tuple-element.7) | copy-start | bytes 18874372
  555.0 12.0 %slice-start.10 = ((s8[6291456]{0:T(1024)(128)(4,1)}), s8[4194304]{0:T(1024)(128)(4,1)S(1)}, s32[]{:S(2)}) async-start(s8[6291456]{0:T(1024)(128)(4,1)} %bitcast.115), calls=%async_computation.17 | async-start | bytes 8388608
  560.0 7.0 %slice-start.11 = ((s8[6291456]{0:T(1024)(128)(4,1)}), s8[2097152]{0:T(1024)(128)(4,1)S(1)}, s32[]{:S(2)}) async-start(s8[6291456]{0:T(1024)(128)(4,1)} %bitcast.115), calls=%async_computation.18 | async-start | bytes 4194304
  565.0 4.1 slice-start
  565.0 6.3 slice-start.8
  567.0 2.2 slice-start.1
  567.1 4.2 slice-start.9
  567.1 6.3 slice-start.6
  569.2 4.1 slice-start.7
  569.2 6.1 slice-start.4
  571.3 4.1 slice-start.5
  573.4 4.1 slice-start.2
  575.4 2.0 slice-start.3
  577.5 78.2 %copy-start.3 = (bf16[8,64,96]{2,1,0:T(8,128)(2,1)S(1)}, bf16[8,64,96]{2,1,0:T(8,128)(2,1)}, u32[]{:S(2)}) copy-start(bf16[8,64,96]{2,1,0:T(8,128)(2,1)} %param.3) | copy-start | bytes 294916
Sparse Core Ops, SparseCore 0:
  20.0 42.9 all-gather.3
  64.7 104.6 all-gather.5
  183.1 63.5 reduce-scatter.2
  248.4 269.5 all-gather.7
  580.4 74.2 reduce-scatter.4
where the time goes:
time: 663 us
  waiting for transfers between devices  547 us (83%)
  local copies, waits for them, and re-layouts  50.4 us (8%)
  matrix products  38.2 us (6%)
  between operations  13.6 us (2%)
  blocking collectives  11.2 us (2%)
    all_gather x1, waiting for transfers between devices, local(): gathered = lax.all_gather(hidden, ('row', 'slab'), axis=0, tiled=True)  269 us
    all_gather x1, waiting for transfers between devices, local(): kernel = lax.all_gather(first_weight, 'slab', axis=2, tiled=True)  96.3 us
    reduce_scatter x1, waiting for transfers between devices, local(): lax.psum_scatter(total.astype(jnp.bfloat16), 'col', scatter_dimension=0,...  74.4 us
    reduce_scatter x1, waiting for transfers between devices, local(): lax.psum_scatter(partial_sum.astype(jnp.bfloat16), 'row', scatter_dimensi...  63.6 us
    all_gather x1, waiting for transfers between devices, local(): channels = lax.all_gather(full_input, 'slab', axis=2, tiled=True)  42.3 us
    slice x1, local copies, waits for them, and re-layouts, local(): padded_hidden[vertical:vertical + lines, sideways:sideways + width, :]  37 us
    dot_general x9, matrix products, local(): jnp.dot(window, second_weight[vertical, sideways], preferred_element_type...  24.7 us
    dot_general x9, matrix products, local(): jnp.dot(chosen, kernel[vertical, sideways], preferred_element_type=jnp.fl...  13.5 us
  transfers between devices with their start and end apart: 5, of which 5 were waited for; matrix products, arithmetic and copies ran while one was open for 2% of the time, Pallas kernels for 0%

commit v1 on v0

v1 whole, which is shorter than its diff:
```python
import functools

import jax
import jax.numpy as jnp
from jax import lax
from jax.experimental import pallas as pl
from jax.experimental.pallas import tpu as pltpu
from jax.sharding import Mesh, PartitionSpec as P


AXES = ("xl", "z", "xh", "core", "y")
H, W, B = 32, 64, 384


def shift(name, by):
    n = lax.axis_size(name)
    return [(i, (i + by) % n) for i in range(n)]


def fill_taps(x_ref, taps, at, width):
    taps[:W, :] = jnp.zeros((W, 3 * width), jnp.bfloat16)
    taps[(H + 1) * W :, :] = jnp.zeros((W, 3 * width), jnp.bfloat16)
    step = 4 * W
    column = lax.broadcasted_iota(jnp.int32, (step, width), 0) % W

    def body(k, carry):
        start = pl.multiple_of(k * step, step)
        x = x_ref[pl.ds(start, step), at : at + width]
        wide = x.astype(jnp.float32)
        rows = pl.ds(pl.multiple_of(start + W, W), step)
        left = jnp.where(column == 0, 0.0, pltpu.roll(wide, 1, 0))
        right = jnp.where(column == W - 1, 0.0, pltpu.roll(wide, step - 1, 0))
        taps[rows, :width] = left.astype(jnp.bfloat16)
        taps[rows, width : 2 * width] = x
        taps[rows, 2 * width :] = right.astype(jnp.bfloat16)
        return carry

    lax.fori_loop(0, H * W // step, body, 0)


EARLY = 256


def partial_sums(taps, kernel, at, width):
    total = None
    for v in range(3):
        part = jnp.dot(
            taps[pl.ds(pl.multiple_of(at + v * W, W), 512), :],
            kernel[3 * v : 3 * v + 3].reshape(3 * width, B),
            preferred_element_type=jnp.float32,
        )
        total = part if total is None else total + part
    return total


def early_kernel(ids, x0, x1, x2, x3, own, p3, p2, out_ref, late_taps, x_ref, taps, kernel, sems):
    copies = []
    for i, piece in enumerate((x0, x1, x2, x3)):
        rows = pl.ds(pl.multiple_of(ids[1 + i] * 512, 512), 512)
        copies.append(pltpu.make_async_copy(piece, x_ref.at[rows, :], sems.at[i]))
    start = pl.multiple_of(ids[0] * B, 128)
    blocks = (
        (own.at[:, :, pl.ds(start, B)], 0, 96),
        (p3, 96, 96),
        (p2.at[:, pl.ds(0, EARLY - 192), :], 192, EARLY - 192),
    )
    for i, (block, at, size) in enumerate(blocks):
        copies.append(
            pltpu.make_async_copy(block, kernel.at[:, pl.ds(at, size), :], sems.at[4 + i])
        )
    for copy in copies:
        copy.start()
    for copy in copies[:4]:
        copy.wait()
    fill_taps(x_ref, taps, 0, EARLY)
    fill_taps(x_ref, late_taps, EARLY, B - EARLY)
    for copy in copies[4:]:
        copy.wait()

    def body(k, carry):
        at = pl.multiple_of(k * 512, 512)
        out_ref[pl.ds(at, 512), :] = partial_sums(taps, kernel, at, EARLY)
        return carry

    lax.fori_loop(0, 4, body, 0)


def late_kernel(p2, p1, before, taps, out_ref, kernel, sems):
    rest = 288 - EARLY
    copies = [
        pltpu.make_async_copy(
            p2.at[:, pl.ds(EARLY - 192, rest), :], kernel.at[:, pl.ds(0, rest), :], sems.at[0]
        ),
        pltpu.make_async_copy(p1, kernel.at[:, pl.ds(rest, 96), :], sems.at[1]),
    ]
    for copy in copies:
        copy.start()
    for copy in copies:
        copy.wait()

    def body(k, carry):
        at = pl.multiple_of(k * 512, 512)
        total = before[pl.ds(at, 512), :] + partial_sums(taps, kernel, at, B - EARLY)
        out_ref[pl.ds(at, 512), :] = total.astype(jnp.bfloat16)
        return carry

    lax.fori_loop(0, 4, body, 0)


def kernel_copies(ids, at, width, own, pieces, kernel, sems):
    start = pl.multiple_of(ids[0] * B + at, 128)
    copies = []
    for s in range(4):
        for b in range(3):
            if s == 0:
                source = own.at[:, b, :, pl.ds(start, width)]
            else:
                source = pieces[s - 1].at[:, b, :, pl.ds(at, width)]
            rows = pl.ds(pl.multiple_of(lax.rem(ids[0] + 4 - s, 4) * 96, 96), 96)
            target = kernel.at[:, rows, pl.ds(b * width, width)]
            copies.append(pltpu.make_async_copy(source, target, sems.at[3 * s + b]))
    return copies


def dots(taps, kernel, at):
    total = None
    for v in range(3):
        part = lax.dot_general(
            kernel[v],
            taps[pl.ds(pl.multiple_of(at + v * W, W), 512), :],
            (((1,), (1,)), ((), ())),
            preferred_element_type=jnp.float32,
        )
        total = part if total is None else total + part
    return total


def second_kernel(width, n, ids, own, p1, p2, p3, *refs):
    pieces, (keep, give, hidden, taps, kernel, sems, wsems) = refs[:n], refs[n:]
    weights = kernel_copies(ids, 0, width, own, (p1, p2, p3), kernel, wsems)
    copies, count = [], 0
    for piece in pieces:
        for j in range(piece.shape[0]):
            rows = pl.ds(pl.multiple_of(ids[2 + count] * 128, 128), 128)
            copies.append(pltpu.make_async_copy(piece.at[j], hidden.at[rows, :], sems.at[count]))
            count += 1
    for copy in weights + copies:
        copy.start()
    for copy in copies:
        copy.wait()
    fill_taps(hidden, taps, 0, width)
    for copy in weights:
        copy.wait()
    core = ids[1]

    def body(h, carry):
        for ref, c in ((keep, core), (give, 1 - core)):
            at = pl.multiple_of((h * 2 + c) * 512, 512)
            ref[pl.ds(h, 1)] = dots(taps, kernel, at).astype(jnp.bfloat16)[None]
        return carry

    lax.fori_loop(0, 2, body, 0)


ANY = pl.BlockSpec(memory_space=pl.ANY)
SMEM = pl.BlockSpec(memory_space=pltpu.SMEM)
VMEM = pl.BlockSpec(memory_space=pltpu.VMEM)
PARAMS = pltpu.CompilerParams(vmem_limit_bytes=40 << 20)


def early_conv(ids, x, own, p3, p2):
    return pl.pallas_call(
        early_kernel,
        out_shape=(
            jax.ShapeDtypeStruct((H * W, B), jnp.float32),
            jax.ShapeDtypeStruct(((H + 2) * W, 3 * (B - EARLY)), jnp.bfloat16),
        ),
        in_specs=[SMEM] + [ANY] * 7,
        out_specs=(VMEM, VMEM),
        scratch_shapes=[
            pltpu.VMEM((H * W, B), jnp.bfloat16),
            pltpu.VMEM(((H + 2) * W, 3 * EARLY), jnp.bfloat16),
            pltpu.VMEM((9, EARLY, B), jnp.bfloat16),
            pltpu.SemaphoreType.DMA((7,)),
        ],
        compiler_params=PARAMS,
        name="early_conv",
    )(ids, *x, own, p3, p2)


def late_conv(p2, p1, before, taps):
    return pl.pallas_call(
        late_kernel,
        out_shape=jax.ShapeDtypeStruct((H * W, B), jnp.bfloat16),
        in_specs=[ANY, ANY, VMEM, VMEM],
        out_specs=VMEM,
        scratch_shapes=[
            pltpu.VMEM((9, B - EARLY, B), jnp.bfloat16),
            pltpu.SemaphoreType.DMA((2,)),
        ],
        compiler_params=PARAMS,
        name="late_conv",
    )(p2, p1, before, taps)


def second_conv(ids, own, weights, pieces):
    n = len(pieces)
    half = jax.ShapeDtypeStruct((2, B, 512), jnp.bfloat16)
    return pl.pallas_call(
        functools.partial(second_kernel, B, n),
        out_shape=(half, half),
        in_specs=[SMEM] + [ANY] * (4 + n),
        out_specs=(VMEM, VMEM),
        scratch_shapes=[
            pltpu.VMEM((H * W, B), jnp.bfloat16),
            pltpu.VMEM(((H + 2) * W, 3 * B), jnp.bfloat16),
            pltpu.VMEM((3, B, 3 * B), jnp.bfloat16),
            pltpu.SemaphoreType.DMA((16,)),
            pltpu.SemaphoreType.DMA((12,)),
        ],
        compiler_params=PARAMS,
        name="second_conv",
    )(ids, own, *weights, *pieces)


def spread(weight, y, at, width):
    out = []
    for s in (1, 3, 2):
        block = lax.dynamic_slice_in_dim(weight, ((y + s) % 4) * B + at, width, weight.ndim - 1)
        out.append(lax.ppermute(block, "y", shift("y", s)))
    return [out[0], out[2], out[1]]


def layer(inputs, first_weight, second_weight):
    y = lax.axis_index("y")
    z = lax.axis_index("z")
    xl = lax.axis_index("xl")
    xh = lax.axis_index("xh")
    core = lax.axis_index("core")
    w1 = first_weight.reshape(9, 96, 4 * B)
    w2 = jnp.transpose(second_weight, (0, 1, 3, 2))

    parts = [inputs] + [lax.ppermute(inputs, "y", shift("y", s)) for s in (3, 2, 1)]
    mine = jnp.concatenate(parts, axis=2).reshape(512, B)
    far = lax.ppermute(mine, "xh", shift("xh", 1))
    near = lax.ppermute(mine, "core", shift("core", 1))
    both = lax.ppermute(far, "core", shift("core", 1))
    x = (mine, near, far, both)
    cols = [2 * xh + core, 2 * xh + 1 - core, 2 - 2 * xh + core, 3 - 2 * xh - core]
    ids = jnp.stack([y] + cols).astype(jnp.int32)

    k1 = spread(w1, y, 0, B)
    k2 = spread(w2, y, 0, B)

    block = H * W // 16
    before, taps = early_conv(ids, x, w1, k1[2], k1[1])
    first = late_conv(k1[1], k1[0], before, taps)
    terms = lax.all_to_all(first.reshape(16, block, B), ("xl", "z"), 0, 0, tiled=True)
    summed = jnp.sum(terms.astype(jnp.float32), axis=0)
    own = jax.nn.silu(summed).astype(jnp.bfloat16)[None]

    near, far, places = [own], [lax.ppermute(own, "xl", shift("xl", 1))], [[z]]
    up = down = own
    for k in range(1, 5):
        up = lax.ppermute(up, "z", shift("z", 1))
        if k < 4:
            down = lax.ppermute(down, "z", shift("z", -1))
            both, at = jnp.concatenate([up, down]), [(z - k) % 8, (z + k) % 8]
        else:
            both, at = up, [(z - k) % 8]
        near.append(both)
        far.append(lax.ppermute(both, "xl", shift("xl", 1)))
        places.append(at)
    flat = [place for at in places for place in at]
    ids = [y, core] + [xl * 8 + place for place in flat] + [(1 - xl) * 8 + place for place in flat]
    keep, give = second_conv(jnp.stack(ids).astype(jnp.int32), w2, k2, near + far)

    got = lax.ppermute(give, "core", shift("core", 1))
    both = (keep.astype(jnp.float32) + got.astype(jnp.float32)).astype(jnp.bfloat16)
    terms = lax.all_to_all(both.reshape(8, 96, 512), ("xh", "y"), 0, 0, tiled=True)
    total = jnp.sum(terms.astype(jnp.float32), axis=0).T
    return (inputs.astype(jnp.float32) + total.reshape(inputs.shape)).astype(jnp.bfloat16)


def solution(mesh):
    fine = Mesh(mesh.devices.reshape(2, 8, 2, 2, 4), AXES)
    row_slab, col = ("xl", "z", "y"), ("xh", "core")
    return jax.shard_map(
        layer,
        mesh=fine,
        in_specs=(P(col, None, row_slab), P(None, None, row_slab, col), P(None, None, col, row_slab)),
        out_specs=P(col, None, row_slab),
        check_vma=False,
    )
```

time: 663 us -> 189 us (0.29)
  waiting for transfers between devices: 547 us -> 52.9 us
  blocking collectives: 11.2 us -> 60.3 us
  local copies, waits for them, and re-layouts: 50.4 us -> 10.1 us
  matrix products: 38.2 us -> 0 us
  starting transfers between devices: 0.35 us -> 37.7 us
  Pallas kernels: 0 us -> 23.2 us
  between operations: 13.6 us -> 0.13 us
    all_gather x3 -> x0, waiting for transfers between devices: 408 us -> none  [the longest x1 269 us: local(): gathered = lax.all_gather(hidden, ('row', 'slab'), axis=0, tiled=True)]
    reduce_scatter x2 -> x0, waiting for transfers between devices: 138 us -> none  [the longest x1 74.4 us: local(): lax.psum_scatter(total.astype(jnp.bfloat16), 'col', scatter_dimension=0,...]
    all_to_all x0 -> x2, blocking collectives: none -> 60.3 us  [the longest x1 44.4 us: layer(): lax.all_to_all(first.reshape(16, block, B), ('xl', 'z'), 0, 0, tiled=True)]
    ppermute x0 -> x25, waiting for transfers between devices: none -> 52.9 us  [the longest x6 24 us: spread(): out.append(lax.ppermute(block, 'y', shift('y', s)))]
    slice x2 -> x0, local copies, waits for them, and re-layouts: 42.1 us -> none  [the longest x1 37 us: local(): padded_hidden[vertical:vertical + lines, sideways:sideways + width, :]]
    dot_general x18 -> x0, matrix products: 38.2 us -> none  [the longest x9 24.7 us: local(): jnp.dot(window, second_weight[vertical, sideways], preferred_element_type...]
    ppermute x0 -> x25, starting transfers between devices: none -> 37.7 us  [the longest x6 9.84 us: spread(): out.append(lax.ppermute(block, 'y', shift('y', s)))]
    pallas_call x0 -> x3, Pallas kernels: none -> 23.2 us  [the longest x1 10 us: second_conv(): pl.pallas_call(functools.partial(second_kernel, B, n), out_shape=(half, h...]
  transfers between devices with their start and end apart: 5 -> 25, of which waited for: 5 -> 17; matrix products, arithmetic and copies ran while one was open for 2% -> 3% of each run, Pallas kernels for 0% -> 4%
where the time goes in v1:
time: 189 us; the launch traced here: 188 us
  blocking collectives  60.3 us (32%)
  waiting for transfers between devices  52.9 us (28%)
  starting transfers between devices  37.7 us (20%)
  Pallas kernels  23.2 us (12%)
  local copies, waits for them, and re-layouts  10.1 us (5%)
  other arithmetic  3.84 us (2%)
    all_to_all x1, blocking collectives, layer(): lax.all_to_all(first.reshape(16, block, B), ('xl', 'z'), 0, 0, tiled=True)  44.4 us
    ppermute x6, waiting for transfers between devices, spread(): out.append(lax.ppermute(block, 'y', shift('y', s)))  24 us
    all_to_all x1, blocking collectives, layer(): lax.all_to_all(both.reshape(8, 96, 512), ('xh', 'y'), 0, 0, tiled=True)  15.9 us
    pallas_call x1, Pallas kernels, second_conv(): pl.pallas_call(functools.partial(second_kernel, B, n), out_shape=(half, h...  10 us
    ppermute x6, starting transfers between devices, spread(): out.append(lax.ppermute(block, 'y', shift('y', s)))  9.84 us
    ppermute x3, waiting for transfers between devices, layer(): lax.ppermute(inputs, 'y', shift('y', s))  8.82 us
    pallas_call x1, Pallas kernels, early_conv(): pl.pallas_call(early_kernel, out_shape=(jax.ShapeDtypeStruct((H * W, B),...  8.41 us
    ppermute x3, waiting for transfers between devices, layer(): down = lax.ppermute(down, 'z', shift('z', -1))  6.19 us
  transfers between devices with their start and end apart: 25, of which 17 were waited for; matrix products, arithmetic and copies ran while one was open for 3% of the time, Pallas kernels for 4%

profile of v1, /device:TPU:1, one launch (start us, length us, event | category | flops | bytes accessed | tf_op | source)
XLA Modules:
  0.0 188.1 jit_solution(8877487563437573841)
XLA Ops:
  0.0 3.6 %collective-permute-start.5 = (bf16[8,64,96]{2,1,0:T(8,128)(2,1)}, bf16[8,64,96]{2,1,0:T(8,128)(2,1)S(1)}, u32[]{:S(2)}, u32[]{:S(2)}) collective-permute-start(bf16[8,64,96]{2,1,0:T(8,128)(2,1)} %param.3), channel_id=1, source_target_pairs={{0,3},{1,0},{2,1},{3,2},{4,7},{5,4},{6,5},{7,6},{8,11},{9,8},{10,9... | collective-permute-start | bytes 294920 | tf_op jit(solution)/shard_map/ppermute | solution.py:243
  3.6 0.3 collective-permute-start.6
  3.9 0.7 collective-permute-start.7
  4.6 3.0 %collective-permute-done.5 = bf16[8,64,96]{2,1,0:T(8,128)(2,1)S(1)} collective-permute-done((bf16[8,64,96]{2,1,0:T(8,128)(2,1)}, bf16[8,64,96]{2,1,0:T(8,128)(2,1)S(1)}, u32[]{:S(2)}, u32[]{:S(2)}) %collective-permute-start.5) | collective-permute-done | bytes 98336 | tf_op jit(solution)/shard_map/ppermute | solution.py:243
  7.5 1.6 collective-permute-done.6
  9.2 4.2 %collective-permute-done.7 = bf16[8,64,96]{2,1,0:T(8,128)(2,1)S(1)} collective-permute-done((bf16[8,64,96]{2,1,0:T(8,128)(2,1)}, bf16[8,64,96]{2,1,0:T(8,128)(2,1)S(1)}, u32[]{:S(2)}, u32[]{:S(2)}) %collective-permute-start.7) | collective-permute-done | bytes 98336 | tf_op jit(solution)/shard_map/ppermute | solution.py:243
  13.4 1.9 %pad_maximum_fusion = bf16[8,64,384]{2,1,0:T(8,128)(2,1)} fusion(bf16[8,64,96]{2,1,0:T(8,128)(2,1)S(1)} %collective-permute-done.7, bf16[8,64,96]{2,1,0:T(8,128)(2,1)S(1)} %collective-permute-done.6, bf16[8,64,96]{2,1,0:T(8,128)(2,1)S(1)} %collective-permute-done.5, bf16[8,64,96]{2,1,0:T(8,128)(2,1)} %param.3), kind=kLoop, calls=%fused_computation.6 | loop fusion | flops 1572864 | bytes 786432 | tf_op jit(solution)/shard_map/concatenate | solution.py:244
  15.3 2.7 %collective-permute-start.9 = (bf16[512,384]{1,0:T(8,128)(2,1)}, bf16[512,384]{1,0:T(8,128)(2,1)}, u32[]{:S(2)}, u32[]{:S(2)}) collective-permute-start(bf16[512,384]{1,0:T(8,128)(2,1)} %bitcast.27.x0), channel_id=1, source_target_pairs={{0,8},{8,0},{1,9},{9,1},{2,10},{10,2},{3,11},{11,3},{4,12},{12,4},... | collective-permute-start | bytes 1179656 | tf_op jit(solution)/shard_map/ppermute | solution.py:245
  18.1 3.0 %constant_dynamic-slice_fusion = (bf16[9,96,384]{2,1,0:T(8,128)(2,1)}, bf16[9,96,384]{2,1,0:T(8,128)(2,1)}, bf16[9,96,384]{2,1,0:T(8,128)(2,1)}) fusion(bf16[9,96,1536]{2,1,0:T(8,128)(2,1)} %bitcast.49, s32[]{:T(128)S(6)} %select_n.73, s32[]{:T(128)S(6)} %select_n.69, s32[]{:T(128)S(6)} %select_n.71), kind=kLoop, calls=%fused_computation.20 | loop fusion | bytes 3981324 | tf_op jit(solution)/shard_map/dynamic_slice | solution.py:229
  21.1 1.5 collective-permute-start.4
  22.6 1.4 collective-permute-start.8
  24.0 3.2 %collective-permute-done.9.x2 = bf16[512,384]{1,0:T(8,128)(2,1)} collective-permute-done((bf16[512,384]{1,0:T(8,128)(2,1)}, bf16[512,384]{1,0:T(8,128)(2,1)}, u32[]{:S(2)}, u32[]{:S(2)}) %collective-permute-start.9) | collective-permute-done | bytes 393248 | tf_op jit(solution)/shard_map/ppermute | solution.py:245
  27.2 1.4 collective-permute-start.10
  28.7 0.1 stack.96.ids
  28.8 8.3 %collective-permute-done.11.p3 = bf16[9,96,384]{2,1,0:T(8,128)(2,1)} collective-permute-done((bf16[9,96,384]{2,1,0:T(8,128)(2,1)}, bf16[9,96,384]{2,1,0:T(8,128)(2,1)}, u32[]{:S(2)}, u32[]{:S(2)}) %collective-permute-start.11) | collective-permute-done | bytes 663584 | tf_op jit(solution)/shard_map/ppermute | solution.py:230
  37.0 0.9 collective-permute-done.3.p2
  37.9 8.4 %early_conv.1 = (f32[2048,384]{1,0:T(8,128)S(1)}, bf16[2176,384]{1,0:T(8,128)(2,1)S(1)}) custom-call(s32[5]{0:T(128)S(1)} %stack.96.ids, bf16[512,384]{1,0:T(8,128)(2,1)} %bitcast.27.x0, bf16[512,384]{1,0:T(8,128)(2,1)} %collective-permute-done.8.x1, bf16[512,384]{1,0:T(8,128)(2,1)} %collective-permute-done.9.x2, ...), custom_call_target="tpu_custom_call" | custom-call | tf_op jit(solution)/shard_map/early_conv/pallas_call | solution.py:172
  46.3 7.6 %collective-permute-done.4.p1 = bf16[9,96,384]{2,1,0:T(8,128)(2,1)} collective-permute-done((bf16[9,96,384]{2,1,0:T(8,128)(2,1)}, bf16[9,96,384]{2,1,0:T(8,128)(2,1)}, u32[]{:S(2)}, u32[]{:S(2)}) %collective-permute-start.4) | collective-permute-done | bytes 663584 | tf_op jit(solution)/shard_map/ppermute | solution.py:230
  54.0 4.8 %late_conv.1 = bf16[2048,384]{1,0:T(8,128)(2,1)S(1)} custom-call(bf16[9,96,384]{2,1,0:T(8,128)(2,1)S(1)} %collective-permute-done.3.p2, bf16[9,96,384]{2,1,0:T(8,128)(2,1)} %collective-permute-done.4.p1, f32[2048,384]{1,0:T(8,128)S(1)} %get-tuple-element.9.before, bf16[2176,384]{1,0:T(8,128)(2,1)S(1)} %get-tuple-element.10.taps), custom_call_target="tpu_custom_call" | custom-call | tf_op jit(solution)/shard_map/late_conv/pallas_call | solution.py:192
  58.8 0.0 copy-start
  58.8 44.4 %all_to_all.10 = bf16[16,128,384]{2,1,0:T(8,128)(2,1)S(1)} all-to-all(bf16[16,128,384]{2,1,0:T(8,128)(2,1)S(1)} %bitcast.51), channel_id=1, replica_groups=mesh['xl'=2,'z'=8,'xh'=2,'core'=2,'y'=4] {'xl','z'}, dimensions={0} | all-to-all | bytes 3145728 | tf_op jit(solution)/shard_map/all_to_all | solution.py:258
  103.2 0.2 convert_reduce_fusion
  103.4 0.7 fusion.3.refs_0_
  104.1 2.4 %collective-permute-start.12 = (bf16[1,128,384]{2,1,0:T(8,128)(2,1)}, bf16[1,128,384]{2,1,0:T(8,128)(2,1)S(1)}, u32[]{:S(2)}, u32[]{:S(2)}) collective-permute-start(bf16[1,128,384]{2,1,0:T(8,128)(2,1)} %fusion.3.refs_0_), channel_id=1, source_target_pairs={{0,16},{16,32},{32,48},{48,64},{64,80},{80,96},{96,112},{112,0},{1... | collective-permute-start | bytes 294920 | tf_op jit(solution)/shard_map/ppermute | solution.py:265
  106.5 0.2 dynamic-slice_bitcast_fusion
  106.7 4.2 %collective-permute-start = (bf16[3,3,96,384]{3,2,1,0:T(8,128)(2,1)S(1)}, bf16[3,3,96,384]{3,2,1,0:T(8,128)(2,1)S(1)}, u32[]{:S(2)}, u32[]{:S(2)}) collective-permute-start(bf16[3,3,96,384]{3,2,1,0:T(8,128)(2,1)S(1)} %get-tuple-element.17), channel_id=1, source_target_pairs={{0,1},{1,2},{2,3},{3,0},{4,5},{5,6},{6,7},{7,4},{8,9},{9,10},{10,1... | collective-permute-start | bytes 1990664 | tf_op jit(solution)/shard_map/ppermute | solution.py:230
  110.9 4.2 %collective-permute-start.1 = (bf16[3,3,96,384]{3,2,1,0:T(8,128)(2,1)S(1)}, bf16[3,3,96,384]{3,2,1,0:T(8,128)(2,1)S(1)}, u32[]{:S(2)}, u32[]{:S(2)}) collective-permute-start(bf16[3,3,96,384]{3,2,1,0:T(8,128)(2,1)S(1)} %get-tuple-element.18), channel_id=1, source_target_pairs={{0,2},{1,3},{2,0},{3,1},{4,6},{5,7},{6,4},{7,5},{8,10},{9,11},{10,... | collective-permute-start | bytes 1990664 | tf_op jit(solution)/shard_map/ppermute | solution.py:230
  115.1 0.7 collective-permute-start.13
  115.8 0.8 collective-permute-start.14
  116.6 0.6 constant_dynamic-update-slice_fusion.1
  117.2 1.9 collective-permute-done.13
  119.1 0.7 constant_dynamic-update-slice_fusion.refs_1_
  119.7 1.3 collective-permute-start.20
  121.1 1.2 collective-permute-start.15
  122.3 0.6 constant_dynamic-update-slice_fusion.3
  122.9 1.9 %collective-permute-done.15 = bf16[1,128,384]{2,1,0:T(8,128)(2,1)S(1)} collective-permute-done((bf16[1,128,384]{2,1,0:T(8,128)(2,1)S(1)}, bf16[1,128,384]{2,1,0:T(8,128)(2,1)S(1)}, u32[]{:S(2)}, u32[]{:S(2)}) %collective-permute-start.15) | collective-permute-done | bytes 98336 | tf_op jit(solution)/shard_map/ppermute | solution.py:267
  124.8 0.7 collective-permute-start.16
  125.6 0.7 constant_dynamic-update-slice_fusion.2.refs_2_
  126.2 3.6 %collective-permute-done.16 = bf16[1,128,384]{2,1,0:T(8,128)(2,1)S(1)} collective-permute-done((bf16[1,128,384]{2,1,0:T(8,128)(2,1)S(1)}, bf16[1,128,384]{2,1,0:T(8,128)(2,1)S(1)}, u32[]{:S(2)}, u32[]{:S(2)}) %collective-permute-start.16) | collective-permute-done | bytes 98336 | tf_op jit(solution)/shard_map/ppermute | solution.py:265
  129.8 1.3 collective-permute-start.17
  131.1 2.4 %collective-permute-done.17 = bf16[1,128,384]{2,1,0:T(8,128)(2,1)S(1)} collective-permute-done((bf16[1,128,384]{2,1,0:T(8,128)(2,1)S(1)}, bf16[1,128,384]{2,1,0:T(8,128)(2,1)S(1)}, u32[]{:S(2)}, u32[]{:S(2)}) %collective-permute-start.17) | collective-permute-done | bytes 98336 | tf_op jit(solution)/shard_map/ppermute | solution.py:267
  133.6 0.4 collective-permute-start.21
  134.0 1.2 collective-permute-start.22
  135.2 6.3 %collective-permute-done.1.p2 = bf16[3,3,96,384]{3,2,1,0:T(8,128)(2,1)S(1)} collective-permute-done((bf16[3,3,96,384]{3,2,1,0:T(8,128)(2,1)S(1)}, bf16[3,3,96,384]{3,2,1,0:T(8,128)(2,1)S(1)}, u32[]{:S(2)}, u32[]{:S(2)}) %collective-permute-start.1) | collective-permute-done | bytes 663584 | tf_op jit(solution)/shard_map/ppermute | solution.py:230
  141.5 0.8 copy-done.2
  142.3 0.8 collective-permute-done.2.p3
  143.2 0.9 copy-done.4
  144.0 1.3 collective-permute-start.19
  145.4 1.8 collective-permute-done.18.refs_4_
  147.1 1.1 collective-permute-start.23
  148.2 0.1 stack.91.ids
  148.3 0.8 collective-permute-done.19.refs_5_
  149.2 2.5 %collective-permute-done.23.refs_9_ = bf16[1,128,384]{2,1,0:T(8,128)(2,1)} collective-permute-done((bf16[1,128,384]{2,1,0:T(8,128)(2,1)}, bf16[1,128,384]{2,1,0:T(8,128)(2,1)}, u32[]{:S(2)}, u32[]{:S(2)}) %collective-permute-start.23) | collective-permute-done | bytes 98336 | tf_op jit(solution)/shard_map/ppermute | solution.py:272
  151.7 1.1 copy-done.3
  152.8 1.1 copy-done.5
  153.9 10.0 %second_conv.1 = (bf16[2,384,512]{2,1,0:T(8,128)(2,1)S(1)}, bf16[2,384,512]{2,1,0:T(8,128)(2,1)S(1)}) custom-call(s32[18]{0:T(128)S(1)} %stack.91.ids, bf16[3,3,96,1536]{3,2,1,0:T(8,128)(2,1)S(1)} %bitcast.48, bf16[3,3,96,384]{3,2,1,0:T(8,128)(2,1)S(1)} %collective-permute-done.p1, bf16[3,3,96,384]{3,2,1,0:T(8,128)(2,1)S(1)} %copy-done.3, ...), custom_call_target="tpu_custom_call" | custom-call | tf_op jit(solution)/shard_map/second_conv/pallas_call | solution.py:209
  163.9 5.2 %collective-permute-start.24 = (bf16[2,384,512]{2,1,0:T(8,128)(2,1)S(1)}, bf16[2,384,512]{2,1,0:T(8,128)(2,1)S(1)}, u32[]{:S(2)}, u32[]{:S(2)}) collective-permute-start(bf16[2,384,512]{2,1,0:T(8,128)(2,1)S(1)} %get-tuple-element.12), channel_id=1, source_target_pairs={{0,4},{4,0},{1,5},{5,1},{2,6},{6,2},{3,7},{7,3},{8,12},{12,8},{9,1... | collective-permute-start | bytes 2359304 | tf_op jit(solution)/shard_map/ppermute | solution.py:278
  169.2 1.9 %collective-permute-done.24 = bf16[2,384,512]{2,1,0:T(8,128)(2,1)S(1)} collective-permute-done((bf16[2,384,512]{2,1,0:T(8,128)(2,1)S(1)}, bf16[2,384,512]{2,1,0:T(8,128)(2,1)S(1)}, u32[]{:S(2)}, u32[]{:S(2)}) %collective-permute-start.24) | collective-permute-done | bytes 786464 | tf_op jit(solution)/shard_map/ppermute | solution.py:278
  171.1 0.2 add_convert_fusion
  171.3 0.0 copy-start.6
  171.3 15.9 %all_to_all.11 = bf16[8,96,512]{2,1,0:T(8,128)(2,1)S(1)} all-to-all(bf16[8,96,512]{2,1,0:T(8,128)(2,1)S(1)} %bitcast.52), channel_id=1, replica_groups=mesh['xl'=2,'z'=8,'xh'=2,'core'=2,'y'=4] {'xh','y'}, dimensions={0} | all-to-all | bytes 1572864 | tf_op jit(solution)/shard_map/all_to_all | solution.py:280
  187.2 0.1 convert_reduce_fusion.1
  187.3 0.1 copy.5
  187.4 0.7 add_convert_fusion.1
  (22 shorter events, 0.1 us)
Async XLA Ops:
  0.0 7.5 %collective-permute-start.5 = (bf16[8,64,96]{2,1,0:T(8,128)(2,1)}, bf16[8,64,96]{2,1,0:T(8,128)(2,1)S(1)}, u32[]{:S(2)}, u32[]{:S(2)}) collective-permute-start(bf16[8,64,96]{2,1,0:T(8,128)(2,1)} %param.3), channel_id=1, source_target_pairs={{0,3},{1,0},{2,1},{3,2},{4,7},{5,4},{6,5},{7,6},{8,11},{9,8},{10,9... | collective-permute-start | bytes 294920 | tf_op jit(solution)/shard_map/ppermute | solution.py:243
  3.6 5.6 %collective-permute-start.6 = (bf16[8,64,96]{2,1,0:T(8,128)(2,1)}, bf16[8,64,96]{2,1,0:T(8,128)(2,1)S(1)}, u32[]{:S(2)}, u32[]{:S(2)}) collective-permute-start(bf16[8,64,96]{2,1,0:T(8,128)(2,1)} %param.3), channel_id=1, source_target_pairs={{0,2},{1,3},{2,0},{3,1},{4,6},{5,7},{6,4},{7,5},{8,10},{9,11},{10,... | collective-permute-start | bytes 294920 | tf_op jit(solution)/shard_map/ppermute | solution.py:243
  3.9 9.5 %collective-permute-start.7 = (bf16[8,64,96]{2,1,0:T(8,128)(2,1)}, bf16[8,64,96]{2,1,0:T(8,128)(2,1)S(1)}, u32[]{:S(2)}, u32[]{:S(2)}) collective-permute-start(bf16[8,64,96]{2,1,0:T(8,128)(2,1)} %param.3), channel_id=1, source_target_pairs={{0,1},{1,2},{2,3},{3,0},{4,5},{5,6},{6,7},{7,4},{8,9},{9,10},{10,1... | collective-permute-start | bytes 294920 | tf_op jit(solution)/shard_map/ppermute | solution.py:243
  15.3 11.9 %collective-permute-start.9 = (bf16[512,384]{1,0:T(8,128)(2,1)}, bf16[512,384]{1,0:T(8,128)(2,1)}, u32[]{:S(2)}, u32[]{:S(2)}) collective-permute-start(bf16[512,384]{1,0:T(8,128)(2,1)} %bitcast.27.x0), channel_id=1, source_target_pairs={{0,8},{8,0},{1,9},{9,1},{2,10},{10,2},{3,11},{11,3},{4,12},{12,4},... | collective-permute-start | bytes 1179656 | tf_op jit(solution)/shard_map/ppermute | solution.py:245
  18.1 19.9 %copy-start.1 = (bf16[3,3,96,1536]{3,2,1,0:T(8,128)(2,1)S(1)}, bf16[3,3,96,1536]{3,2,1,0:T(8,128)(2,1)}, u32[]{:S(2)}) copy-start(bf16[3,3,96,1536]{3,2,1,0:T(8,128)(2,1)} %param.4) | copy-start | bytes 7962628
  21.1 15.9 %collective-permute-start.11 = (bf16[9,96,384]{2,1,0:T(8,128)(2,1)}, bf16[9,96,384]{2,1,0:T(8,128)(2,1)}, u32[]{:S(2)}, u32[]{:S(2)}) collective-permute-start(bf16[9,96,384]{2,1,0:T(8,128)(2,1)} %get-tuple-element.13), channel_id=1, source_target_pairs={{0,3},{1,0},{2,1},{3,2},{4,7},{5,4},{6,5},{7,6},{8,11},{9,8},{10,9... | collective-permute-start | bytes 1990664 | tf_op jit(solution)/shard_map/ppermute | solution.py:230
  21.1 16.8 %collective-permute-start.3 = (bf16[9,96,384]{2,1,0:T(8,128)(2,1)}, bf16[9,96,384]{2,1,0:T(8,128)(2,1)S(1)}, u32[]{:S(2)}, u32[]{:S(2)}) collective-permute-start(bf16[9,96,384]{2,1,0:T(8,128)(2,1)} %get-tuple-element.15), channel_id=1, source_target_pairs={{0,2},{1,3},{2,0},{3,1},{4,6},{5,7},{6,4},{7,5},{8,10},{9,11},{10,... | collective-permute-start | bytes 1990664 | tf_op jit(solution)/shard_map/ppermute | solution.py:230
  21.1 32.9 %collective-permute-start.4 = (bf16[9,96,384]{2,1,0:T(8,128)(2,1)}, bf16[9,96,384]{2,1,0:T(8,128)(2,1)}, u32[]{:S(2)}, u32[]{:S(2)}) collective-permute-start(bf16[9,96,384]{2,1,0:T(8,128)(2,1)} %get-tuple-element.14), channel_id=1, source_target_pairs={{0,1},{1,2},{2,3},{3,0},{4,5},{5,6},{6,7},{7,4},{8,9},{9,10},{10,1... | collective-permute-start | bytes 1990664 | tf_op jit(solution)/shard_map/ppermute | solution.py:230
  22.6 6.2 %collective-permute-start.8 = (bf16[512,384]{1,0:T(8,128)(2,1)}, bf16[512,384]{1,0:T(8,128)(2,1)}, u32[]{:S(2)}, u32[]{:S(2)}) collective-permute-start(bf16[512,384]{1,0:T(8,128)(2,1)} %bitcast.27.x0), channel_id=1, source_target_pairs={{0,4},{4,0},{1,5},{5,1},{2,6},{6,2},{3,7},{7,3},{8,12},{12,8},{9,1... | collective-permute-start | bytes 1179656 | tf_op jit(solution)/shard_map/ppermute | solution.py:246
  27.2 10.7 %collective-permute-start.10 = (bf16[512,384]{1,0:T(8,128)(2,1)}, bf16[512,384]{1,0:T(8,128)(2,1)}, u32[]{:S(2)}, u32[]{:S(2)}) collective-permute-start(bf16[512,384]{1,0:T(8,128)(2,1)} %collective-permute-done.9.x2), channel_id=1, source_target_pairs={{0,4},{4,0},{1,5},{5,1},{2,6},{6,2},{3,7},{7,3},{8,12},{12,8},{9,1... | collective-permute-start | bytes 1179656 | tf_op jit(solution)/shard_map/ppermute | solution.py:247
  58.8 47.8 %copy-start = (bf16[3,3,1536,96]{2,3,1,0:T(8,128)(2,1)S(1)}, bf16[3,3,1536,96]{2,3,1,0:T(8,128)(2,1)}, u32[]{:S(2)}) copy-start(bf16[3,3,1536,96]{2,3,1,0:T(8,128)(2,1)} %param.5) | copy-start | bytes 7962628
  104.1 11.7 %collective-permute-start.12 = (bf16[1,128,384]{2,1,0:T(8,128)(2,1)}, bf16[1,128,384]{2,1,0:T(8,128)(2,1)S(1)}, u32[]{:S(2)}, u32[]{:S(2)}) collective-permute-start(bf16[1,128,384]{2,1,0:T(8,128)(2,1)} %fusion.3.refs_0_), channel_id=1, source_target_pairs={{0,16},{16,32},{32,48},{48,64},{64,80},{80,96},{96,112},{112,0},{1... | collective-permute-start | bytes 294920 | tf_op jit(solution)/shard_map/ppermute | solution.py:265
  106.7 27.3 %collective-permute-start = (bf16[3,3,96,384]{3,2,1,0:T(8,128)(2,1)S(1)}, bf16[3,3,96,384]{3,2,1,0:T(8,128)(2,1)S(1)}, u32[]{:S(2)}, u32[]{:S(2)}) collective-permute-start(bf16[3,3,96,384]{3,2,1,0:T(8,128)(2,1)S(1)} %get-tuple-element.17), channel_id=1, source_target_pairs={{0,1},{1,2},{2,3},{3,0},{4,5},{5,6},{6,7},{7,4},{8,9},{9,10},{10,1... | collective-permute-start | bytes 1990664 | tf_op jit(solution)/shard_map/ppermute | solution.py:230
  110.9 30.6 %collective-permute-start.1 = (bf16[3,3,96,384]{3,2,1,0:T(8,128)(2,1)S(1)}, bf16[3,3,96,384]{3,2,1,0:T(8,128)(2,1)S(1)}, u32[]{:S(2)}, u32[]{:S(2)}) collective-permute-start(bf16[3,3,96,384]{3,2,1,0:T(8,128)(2,1)S(1)} %get-tuple-element.18), channel_id=1, source_target_pairs={{0,2},{1,3},{2,0},{3,1},{4,6},{5,7},{6,4},{7,5},{8,10},{9,11},{10,... | collective-permute-start | bytes 1990664 | tf_op jit(solution)/shard_map/ppermute | solution.py:230
  115.1 28.1 %collective-permute-start.2 = (bf16[3,3,96,384]{3,2,1,0:T(8,128)(2,1)S(1)}, bf16[3,3,96,384]{3,2,1,0:T(8,128)(2,1)S(1)}, u32[]{:S(2)}, u32[]{:S(2)}) collective-permute-start(bf16[3,3,96,384]{3,2,1,0:T(8,128)(2,1)S(1)} %get-tuple-element.16), channel_id=1, source_target_pairs={{0,3},{1,0},{2,1},{3,2},{4,7},{5,4},{6,5},{7,6},{8,11},{9,8},{10,9... | collective-permute-start | bytes 1990664 | tf_op jit(solution)/shard_map/ppermute | solution.py:230
  115.1 4.0 %collective-permute-start.13 = (bf16[1,128,384]{2,1,0:T(8,128)(2,1)}, bf16[1,128,384]{2,1,0:T(8,128)(2,1)S(1)}, u32[]{:S(2)}, u32[]{:S(2)}) collective-permute-start(bf16[1,128,384]{2,1,0:T(8,128)(2,1)} %fusion.3.refs_0_), channel_id=1, source_target_pairs={{0,112},{16,0},{32,16},{48,32},{64,48},{80,64},{96,80},{112,96},{1... | collective-permute-start | bytes 294920 | tf_op jit(solution)/shard_map/ppermute | solution.py:267
  115.8 5.3 %collective-permute-start.14 = (bf16[1,128,384]{2,1,0:T(8,128)(2,1)S(1)}, bf16[1,128,384]{2,1,0:T(8,128)(2,1)S(1)}, u32[]{:S(2)}, u32[]{:S(2)}) collective-permute-start(bf16[1,128,384]{2,1,0:T(8,128)(2,1)S(1)} %collective-permute-done.12), channel_id=1, source_target_pairs={{0,16},{16,32},{32,48},{48,64},{64,80},{80,96},{96,112},{112,0},{1... | collective-permute-start | bytes 294920 | tf_op jit(solution)/shard_map/ppermute | solution.py:265
  119.7 29.4 %collective-permute-start.20 = (bf16[2,128,384]{2,1,0:T(8,128)(2,1)}, bf16[2,128,384]{2,1,0:T(8,128)(2,1)}, u32[]{:S(2)}, u32[]{:S(2)}) collective-permute-start(bf16[2,128,384]{2,1,0:T(8,128)(2,1)} %constant_dynamic-update-slice_fusion.refs_1_), channel_id=1, source_target_pairs={{0,128},{128,0},{1,129},{129,1},{2,130},{130,2},{3,131},{131,3},{4... | collective-permute-start | bytes 589832 | tf_op jit(solution)/shard_map/ppermute | solution.py:272
  121.1 3.8 %collective-permute-start.15 = (bf16[1,128,384]{2,1,0:T(8,128)(2,1)S(1)}, bf16[1,128,384]{2,1,0:T(8,128)(2,1)S(1)}, u32[]{:S(2)}, u32[]{:S(2)}) collective-permute-start(bf16[1,128,384]{2,1,0:T(8,128)(2,1)S(1)} %collective-permute-done.13), channel_id=1, source_target_pairs={{0,112},{16,0},{32,16},{48,32},{64,48},{80,64},{96,80},{112,96},{1... | collective-permute-start | bytes 294920 | tf_op jit(solution)/shard_map/ppermute | solution.py:267
  124.8 5.0 %collective-permute-start.16 = (bf16[1,128,384]{2,1,0:T(8,128)(2,1)S(1)}, bf16[1,128,384]{2,1,0:T(8,128)(2,1)S(1)}, u32[]{:S(2)}, u32[]{:S(2)}) collective-permute-start(bf16[1,128,384]{2,1,0:T(8,128)(2,1)S(1)} %collective-permute-done.14), channel_id=1, source_target_pairs={{0,16},{16,32},{32,48},{48,64},{64,80},{80,96},{96,112},{112,0},{1... | collective-permute-start | bytes 294920 | tf_op jit(solution)/shard_map/ppermute | solution.py:265
  129.8 3.8 %collective-permute-start.17 = (bf16[1,128,384]{2,1,0:T(8,128)(2,1)S(1)}, bf16[1,128,384]{2,1,0:T(8,128)(2,1)S(1)}, u32[]{:S(2)}, u32[]{:S(2)}) collective-permute-start(bf16[1,128,384]{2,1,0:T(8,128)(2,1)S(1)} %collective-permute-done.15), channel_id=1, source_target_pairs={{0,112},{16,0},{32,16},{48,32},{64,48},{80,64},{96,80},{112,96},{1... | collective-permute-start | bytes 294920 | tf_op jit(solution)/shard_map/ppermute | solution.py:267
  133.6 15.6 %collective-permute-start.21 = (bf16[2,128,384]{2,1,0:T(8,128)(2,1)}, bf16[2,128,384]{2,1,0:T(8,128)(2,1)}, u32[]{:S(2)}, u32[]{:S(2)}) collective-permute-start(bf16[2,128,384]{2,1,0:T(8,128)(2,1)} %constant_dynamic-update-slice_fusion.2.refs_2_), channel_id=1, source_target_pairs={{0,128},{128,0},{1,129},{129,1},{2,130},{130,2},{3,131},{131,3},{4... | collective-permute-start | bytes 589832 | tf_op jit(solution)/shard_map/ppermute | solution.py:272
  134.0 15.2 %collective-permute-start.22 = (bf16[2,128,384]{2,1,0:T(8,128)(2,1)S(1)}, bf16[2,128,384]{2,1,0:T(8,128)(2,1)}, u32[]{:S(2)}, u32[]{:S(2)}) collective-permute-start(bf16[2,128,384]{2,1,0:T(8,128)(2,1)S(1)} %constant_dynamic-update-slice_fusion.4.refs_3_), channel_id=1, source_target_pairs={{0,128},{128,0},{1,129},{129,1},{2,130},{130,2},{3,131},{131,3},{4... | collective-permute-start | bytes 589832 | tf_op jit(solution)/shard_map/ppermute | solution.py:272
  141.5 0.8 copy-start.2
  142.3 4.8 %collective-permute-start.18 = (bf16[1,128,384]{2,1,0:T(8,128)(2,1)S(1)}, bf16[1,128,384]{2,1,0:T(8,128)(2,1)}, u32[]{:S(2)}, u32[]{:S(2)}) collective-permute-start(bf16[1,128,384]{2,1,0:T(8,128)(2,1)S(1)} %collective-permute-done.16), channel_id=1, source_target_pairs={{0,16},{16,32},{32,48},{48,64},{64,80},{80,96},{96,112},{112,0},{1... | collective-permute-start | bytes 294920 | tf_op jit(solution)/shard_map/ppermute | solution.py:265
  143.2 0.9 copy-start.4
  144.0 5.1 %collective-permute-start.19 = (bf16[1,128,384]{2,1,0:T(8,128)(2,1)}, bf16[1,128,384]{2,1,0:T(8,128)(2,1)}, u32[]{:S(2)}, u32[]{:S(2)}) collective-permute-start(bf16[1,128,384]{2,1,0:T(8,128)(2,1)} %fusion.3.refs_0_), channel_id=1, source_target_pairs={{0,128},{128,0},{1,129},{129,1},{2,130},{130,2},{3,131},{131,3},{4... | collective-permute-start | bytes 294920 | tf_op jit(solution)/shard_map/ppermute | solution.py:262
  147.1 4.6 %collective-permute-start.23 = (bf16[1,128,384]{2,1,0:T(8,128)(2,1)}, bf16[1,128,384]{2,1,0:T(8,128)(2,1)}, u32[]{:S(2)}, u32[]{:S(2)}) collective-permute-start(bf16[1,128,384]{2,1,0:T(8,128)(2,1)} %collective-permute-done.18.refs_4_), channel_id=1, source_target_pairs={{0,128},{128,0},{1,129},{129,1},{2,130},{130,2},{3,131},{131,3},{4... | collective-permute-start | bytes 294920 | tf_op jit(solution)/shard_map/ppermute | solution.py:272
  151.7 1.1 copy-start.3
  152.8 1.1 copy-start.5
  163.9 7.2 %collective-permute-start.24 = (bf16[2,384,512]{2,1,0:T(8,128)(2,1)S(1)}, bf16[2,384,512]{2,1,0:T(8,128)(2,1)S(1)}, u32[]{:S(2)}, u32[]{:S(2)}) collective-permute-start(bf16[2,384,512]{2,1,0:T(8,128)(2,1)S(1)} %get-tuple-element.12), channel_id=1, source_target_pairs={{0,4},{4,0},{1,5},{5,1},{2,6},{6,2},{3,7},{7,3},{8,12},{12,8},{9,1... | collective-permute-start | bytes 2359304 | tf_op jit(solution)/shard_map/ppermute | solution.py:278
  171.3 16.1 %copy-start.6 = (bf16[8,64,96]{2,1,0:T(8,128)(2,1)S(1)}, bf16[8,64,96]{2,1,0:T(8,128)(2,1)}, u32[]{:S(2)}) copy-start(bf16[8,64,96]{2,1,0:T(8,128)(2,1)} %param.3) | copy-start | bytes 294916
